TPU v7x, 32 devices: a whole 2x2x4 slice. The times are simulated.
32 devices in a mesh: groups: 2 (over y), seq: 4 (over z), head: 2 (over x), rep: 2 (over core).
Axes of the slice: x: 2, y: 2, z: 4, core: 2. Of those that a mesh axis runs over, the one named last changes fastest.
Arguments:
- book_tokens: bfloat16 [16384, 1024], P(('groups', 'seq', 'rep')), parts along dimension 0, may hold values from -6 to 6
- norm_gain: float32 [1024], replicated, may hold values from 0.1 to 1.9
- query_weight: bfloat16 [1024, 1024], P(None, 'head'), may hold values from -0.1875 to 0.1875
- key_weight: bfloat16 [1024, 1024], P(None, 'head'), may hold values from -0.1875 to 0.1875
- value_weight: bfloat16 [1024, 1024], P(None, 'head'), may hold values from -0.1875 to 0.1875
- proj_weight: bfloat16 [1024, 4096], P(None, 'head'), may hold values from -0.75 to 0.75
- dual_gains: float32 [4, 1024], P(None, 'head'), may hold values from 0.1 to 1.9
- out_weight: bfloat16 [1024, 1024], P(None, 'head'), may hold values from -1.5 to 1.5
- span_bounds: int32 [128, 2], P('groups'), parts along dimension 0, may hold values from 0 to 8192, as said below
Outputs:
- attended: bfloat16 [16384, 1024], P(('groups', 'seq', 'rep'), 'head'), parts along dimension 0
- pooled: float32 [128, 1024], P(('groups', 'seq', 'rep'), 'head'), parts along dimension 0
There are 2 independent parts, one for each index of `groups`. A program takes and returns all parts, laid end to end along the dimension named above; an argument that names none is the same for every part. Nothing has to cross between parts.
Inputs may be any that keep to these rules, and one draw needn't show every extreme that they name: `span_bounds`: each span lies inside the book and holds 1 to 512 tokens; spans may intersect and come in any order; the longest holds exactly 512 tokens.
All inputs are finite; a program needn't handle non-finite values.
Results may differ from a plain program's by a relative error of at most 0.023.
Values may be sent and summed in bfloat16 or wider, within the bound.
No kernel may reach another device: no remote copies, remote signals or barrier semaphores. Data moves between devices by JAX's collectives and lax.ppermute only.
A program may use at most 64 MiB of HBM per device.

v0:
```python
import jax
import jax.numpy as jnp
from jax import lax
from jax.sharding import PartitionSpec as P

DH = 64
R = 256
SEG = 128
softcap = 5.0
epsilon = 1e-05


def with_halo(cells, sides, width):
    for axis, dim in sides:
        count = lax.axis_size(axis)
        ends = count - 1
        head = lax.slice_in_dim(cells, 0, width, axis=dim)
        tail = lax.slice_in_dim(cells, cells.shape[dim] - width, cells.shape[dim], axis=dim)
        cells = jnp.concatenate(
            [
                lax.ppermute(tail, axis, [(i, (i + 1) % count) for i in range(ends)]),
                cells,
                lax.ppermute(head, axis, [((i + 1) % count, i) for i in range(ends)]),
            ],
            axis=dim,
        )
    return cells


def normalize(values, gain_row):
    centre = jnp.mean(values, axis=-1, keepdims=True)
    spread = jnp.mean(jnp.square(values - centre), axis=-1, keepdims=True)
    return (values - centre) * lax.rsqrt(spread + epsilon) * gain_row


def capped(values):
    return softcap * jnp.tanh(values / softcap)


def finish(total_numer, gain_rows):
    land_keys = normalize(total_numer[:, :, :DH], gain_rows[2][:, None, :])
    land_values = normalize(total_numer[:, :, DH:], gain_rows[3][:, None, :])
    return jnp.concatenate([land_keys, land_values], axis=-1).astype(jnp.bfloat16)


def per_device(
    book_tokens,
    norm_gain,
    query_weight,
    key_weight,
    value_weight,
    proj_weight,
    dual_gains,
    out_weight,
    span_bounds,
):
    tok_rows = book_tokens.shape[0]
    seq_devices = lax.axis_size(("seq", "rep"))
    seq_index = lax.axis_index(("seq", "rep"))
    first_row = seq_index * tok_rows
    length = tok_rows * seq_devices
    head_local = query_weight.shape[1] // DH
    normed = normalize(book_tokens.astype(jnp.float32), norm_gain).astype(jnp.bfloat16)
    queries = jnp.dot(normed, query_weight, preferred_element_type=jnp.float32).astype(jnp.bfloat16)
    queries = queries.reshape(tok_rows, head_local, DH)
    key_raw = jnp.dot(normed, key_weight, preferred_element_type=jnp.float32).reshape(
        tok_rows, head_local, DH
    )
    value_raw = jnp.dot(normed, value_weight, preferred_element_type=jnp.float32).reshape(
        tok_rows, head_local, DH
    )
    gain_rows = dual_gains.reshape(4, head_local, DH)
    near_pairs = jnp.concatenate(
        [normalize(key_raw, gain_rows[0]), normalize(value_raw, gain_rows[1])], axis=-1
    )
    near_pairs = near_pairs.astype(jnp.bfloat16)
    raw_pairs = jnp.concatenate([key_raw, value_raw], axis=-1).astype(jnp.bfloat16)
    logits = jnp.dot(normed, proj_weight, preferred_element_type=jnp.float32)
    proj_weights = jnp.exp(capped(logits)).astype(jnp.bfloat16).reshape(tok_rows, head_local, R)
    numerator = jnp.einsum(
        "nhr,nhe->hre", proj_weights, raw_pairs, preferred_element_type=jnp.float32
    )
    flat_pairs = near_pairs.reshape(tok_rows, head_local * 2 * DH)
    padded = with_halo(flat_pairs, ((("seq", "rep"), 0),), SEG // 2)
    segments = tok_rows // SEG
    blocks = padded.reshape(segments + 1, SEG, head_local, 2 * DH)
    window = jnp.concatenate([blocks[:-1], blocks[1:]], axis=1)
    position = (
        first_row + jnp.arange(segments)[:, None] * SEG + jnp.arange(2 * SEG)[None, :] - SEG // 2
    )
    inside = (position >= 0) & (position < length)
    query_blocks = queries.reshape(segments, SEG, head_local, DH)
    near_scores = jnp.einsum(
        "sqhd,skhd->shqk", query_blocks, window[..., :DH], preferred_element_type=jnp.float32
    )
    near_exp = jnp.where(inside[:, None, None, :], jnp.exp(capped(near_scores * DH ** (-0.5))), 0.0)
    total_numer = lax.psum(numerator.astype(jnp.bfloat16), ("seq", "rep")).astype(jnp.float32)
    land_pairs = finish(total_numer, gain_rows)
    far_scores = jnp.einsum(
        "sqhd,hrd->shqr", query_blocks, land_pairs[..., :DH], preferred_element_type=jnp.float32
    )
    far_exp = jnp.exp(capped(far_scores * DH ** (-0.5)))
    summed = jnp.sum(near_exp, axis=-1, keepdims=True) + jnp.sum(far_exp, axis=-1, keepdims=True)
    near_probs = (near_exp / summed).astype(jnp.bfloat16)
    far_probs = (far_exp / summed).astype(jnp.bfloat16)
    output = jnp.einsum(
        "shqk,skhd->sqhd", near_probs, window[..., DH:], preferred_element_type=jnp.float32
    )
    output = output + jnp.einsum(
        "shqr,hrd->sqhd", far_probs, land_pairs[..., DH:], preferred_element_type=jnp.float32
    )
    heads_out = output.astype(jnp.bfloat16).reshape(tok_rows, head_local * DH)
    projected = jnp.dot(
        lax.all_gather(heads_out, "head", axis=1, tiled=True),
        out_weight,
        preferred_element_type=jnp.float32,
    )
    attended = projected.astype(jnp.bfloat16)
    span_start = span_bounds[:, 0]
    span_end = span_bounds[:, 1]
    position_rows = first_row + jnp.arange(tok_rows)
    member = (position_rows[None, :] >= span_start[:, None]) & (
        position_rows[None, :] < span_end[:, None]
    )
    partial_sums = jnp.dot(
        member.astype(jnp.bfloat16), attended, preferred_element_type=jnp.float32
    )
    own_sums = lax.psum_scatter(
        partial_sums.astype(jnp.bfloat16), ("seq", "rep"), scatter_dimension=0, tiled=True
    ).astype(jnp.float32)
    span_rows = own_sums.shape[0]
    own_bounds = lax.dynamic_slice_in_dim(span_bounds, seq_index * span_rows, span_rows, 0)
    own_counts = (own_bounds[:, 1] - own_bounds[:, 0]).astype(jnp.float32)
    pooled = own_sums / own_counts[:, None]
    return (attended, pooled)


def solution(mesh):
    placed = (
        P(("groups", "seq", "rep"), None),
        P(),
        P(None, "head"),
        P(None, "head"),
        P(None, "head"),
        P(None, "head"),
        P(None, "head"),
        P(None, "head"),
        P("groups", None),
    )
    return jax.shard_map(
        per_device,
        mesh=mesh,
        in_specs=placed,
        out_specs=(P(("groups", "seq", "rep"), "head"), P(("groups", "seq", "rep"), "head")),
        check_vma=False,
    )
```

profile of v0, /device:TPU:0, one launch (start us, length us, event | category | flops | bytes accessed | tf_op | source)
XLA Modules:
  0.0 200.5 jit_solution(12161471431930354215)
XLA Ops:
  7.2 2.1 %convert_reduce_fusion = f32[1024]{0:T(1024)S(1)} fusion(bf16[1024,1024]{1,0:T(8,128)(2,1)} %param.9), kind=kLoop, calls=%fused_computation.9 | loop fusion | flops 2096128 | bytes 2101248 | tf_op jit(solution)/shard_map/reduce_sum | solution.py:31
  10.9 2.3 %bitcast_convert_fusion = (bf16[1024,8,64]{0,2,1:T(8,128)(2,1)}, f32[1024,512]{0,1:T(8,128)S(1)}) fusion(bf16[1024,1024]{1,0:T(8,128)(2,1)S(1)} %fusion.6, bf16[1024,512]{1,0:T(8,128)(2,1)S(1)} %copy-done), kind=kOutput, calls=%fused_computation.34 | convolution fusion | flops 1074266112 | bytes 6291456 | tf_op jit(solution)/shard_map/dot_general | solution.py:69
  14.4 2.3 %bitcast_convert_fusion.1 = (bf16[1024,8,64]{0,2,1:T(8,128)(2,1)}, f32[1024,512]{0,1:T(8,128)S(1)}) fusion(bf16[1024,1024]{1,0:T(8,128)(2,1)S(1)} %fusion.6, bf16[1024,512]{1,0:T(8,128)(2,1)S(1)} %copy-done.15), kind=kOutput, calls=%fused_computation.37 | convolution fusion | flops 1074266112 | bytes 6291456 | tf_op jit(solution)/shard_map/dot_general | solution.py:66
  18.3 2.2 %multiply_multiply_fusion = (bf16[1024,8,64]{0,2,1:T(8,128)(2,1)S(1)}, bf16[1024,8,64]{0,2,1:T(8,128)(2,1)S(1)}) fusion(f32[1024,512]{0,1:T(8,128)S(1)} %get-tuple-element.17, f32[8,64]{1,0:T(8,128)S(1)} %mul.128, f32[1024,8]{0,1:T(8,128)S(1)} %add_rsqrt_fusion, f32[1024,8]{0,1:T(8,128)S(1)} %broadcast_multiply_fusion, f32[8,64]{1,0:T(8,128)S(1)} %mul.123, ...), kind=kLoop, calls=%fused_computation.40 | loop fusion | flops 4194304 | bytes 6426624 | tf_op jit(solution)/shard_map/mul | solution.py:33
  21.0 2.4 %collective-permute-start = (bf16[64,1024]{1,0:T(8,128)(2,1)S(1)}, bf16[64,1024]{1,0:T(8,128)(2,1)S(1)}, u32[]{:S(2)}, u32[]{:S(2)}) collective-permute-start(bf16[64,1024]{1,0:T(8,128)(2,1)S(1)} %copy.38), channel_id=1, source_target_pairs={{0,1},{1,4},{4,5},{5,8},{8,9},{9,12},{12,13},{2,3},{3,6},{6,7},{7,... | collective-permute-start | bytes 393224 | tf_op jit(solution)/shard_map/ppermute | solution.py:21
  25.6 9.9 %exponential_convert_fusion = bf16[1024,2048]{1,0:T(8,128)(2,1)} fusion(bf16[1024,1024]{1,0:T(8,128)(2,1)} %copy-done.6, bf16[1024,2048]{1,0:T(8,128)(2,1)} %param.14), kind=kOutput, calls=%fused_computation.5 | convolution fusion | flops 4301258752 | bytes 10485760 | tf_op jit(solution)/shard_map/dot_general | solution.py:78
  35.6 6.5 %copy.58 = bf16[1024,2048]{0,1:T(8,128)(2,1)} copy(bf16[1024,2048]{1,0:T(8,128)(2,1)} %exponential_convert_fusion) | data formatting | bytes 8388608 | tf_op jit(solution)/shard_map/reshape | solution.py:79
  42.1 4.5 %fusion.23 = bf16[8,256,128]{2,1,0:T(8,128)(2,1)} fusion(bf16[1024,8,256]{0,2,1:T(8,128)(2,1)} %bitcast.78, bf16[1024,8,64]{0,2,1:T(8,128)(2,1)S(1)} %copy-done.17, bf16[1024,8,64]{0,2,1:T(8,128)(2,1)} %get-tuple-element.18), kind=kOutput, calls=%fused_computation.46 | convolution fusion | flops 541327360 | bytes 6815744 | tf_op jit(solution)/shard_map/nhr,nhe->hre/dot_general | solution.py:80
  46.9 2.6 %copy.39 = bf16[1024,1024]{1,0:T(8,128)(2,1)} copy(bf16[1024,1024]{0,1:T(8,128)(2,1)S(1)} %bitcast.75) | data formatting | bytes 4194304 | tf_op jit(solution)/shard_map/convert_element_type | solution.py:76
  49.5 3.1 %convolution_convert_fusion.1 = bf16[1024,512]{1,0:T(8,128)(2,1)S(1)} fusion(bf16[1024,1024]{1,0:T(8,128)(2,1)} %copy-done.6, bf16[1024,512]{1,0:T(8,128)(2,1)} %param.11), kind=kOutput, calls=%fused_computation.45 | convolution fusion | flops 1074266112 | bytes 4194304 | tf_op jit(solution)/shard_map/dot_general | solution.py:64
  52.6 2.1 %reshape.140 = bf16[8,128,8,64]{3,2,1,0:T(8,128)(2,1)} reshape(bf16[1024,512]{1,0:T(8,128)(2,1)S(1)} %convolution_convert_fusion.1) | data formatting | bytes 2097152 | tf_op jit(solution)/shard_map/reshape;reshape | solution.py:92
  54.7 2.4 %copy.45 = bf16[8,128,8,64]{1,3,2,0:T(8,128)(2,1)S(1)} copy(bf16[8,128,8,64]{3,2,1,0:T(8,128)(2,1)} %reshape.140) | data formatting | bytes 2097152 | tf_op jit(solution)/shard_map/reshape;reshape | solution.py:92
  59.3 2.0 copy.64
  61.2 4.3 %copy.42 = bf16[8,128,8,128]{1,3,2,0:T(8,128)(2,1)} copy(bf16[8,128,8,128]{3,2,1,0:T(8,128)(2,1)} %bitcast.76) | data formatting | bytes 4194304 | tf_op jit(solution)/shard_map/slice | solution.py:87
  65.5 1.9 copy.65
  67.5 4.3 %copy.43 = bf16[8,128,8,128]{1,3,2,0:T(8,128)(2,1)} copy(bf16[8,128,8,128]{3,2,1,0:T(8,128)(2,1)} %bitcast.77) | data formatting | bytes 4194304 | tf_op jit(solution)/shard_map/slice | solution.py:87
  71.7 7.5 %fusion.1 = (f32[8,8,128]{2,1,0:T(8,128)S(1)}, f32[8,8,128,256]{3,2,1,0:T(8,128)}) fusion(pred[8,256]{1,0:T(8,128)(4,1)S(1)} %fusion.45, bf16[8,128,8,64]{1,3,2,0:T(8,128)(2,1)S(1)} %copy.45, bf16[8,128,8,128]{1,3,2,0:T(8,128)(2,1)} %copy.43, bf16[8,128,8,128]{1,3,2,0:T(8,128)(2,1)S(1)} %copy-done.7), kind=kOutput, calls=%fused_computation.7 | convolution fusion | flops 281010176 | bytes 13666304 | tf_op jit(solution)/shard_map/sqhd,skhd->shqk/dot_general | solution.py:93
  79.2 28.3 %all-reduce.2.cloned.1.call-done = bf16[8,256,128]{2,1,0:T(8,128)(2,1)} async-done(((bf16[8,256,128]{2,1,0:T(8,128)(2,1)}), bf16[8,256,128]{2,1,0:T(8,128)(2,1)}) %all-reduce.2.cloned.1.call-update) | async-done | bytes 524304 | tf_op jit(solution)/shard_map/psum | solution.py:97
  111.2 3.9 %bitcast_reduce_fusion = (f32[8,8,128]{2,1,0:T(8,128)S(1)}, f32[8,256,8,128]{1,3,0,2:T(8,128)S(1)}) fusion(bf16[8,128,8,64]{1,3,2,0:T(8,128)(2,1)S(1)} %copy-done.10, f32[8,256,128]{2,1,0:T(8,128)S(1)} %convert_element_type.57, f32[8,64]{1,0:T(8,128)S(1)} %mul.138, f32[8,256]{1,0:T(8,128)S(1)} %add_rsqrt_fusion.3, f32[8,256]{1,0:T(8,128)S(1)} %get-tuple-element.25), kind=kOutput, calls=%fused_computation.1 | convolution fusion | flops 275243008 | bytes 10536960 | tf_op jit(solution)/shard_map/sqhd,hrd->shqr/dot_general | solution.py:99
  115.2 5.2 %fusion.8 = f32[8,64,8,128]{3,1,0,2:T(8,128)S(1)} fusion(f32[8,256,8,128]{1,3,0,2:T(8,128)S(1)} %get-tuple-element.23, f32[8,8,128]{2,1,0:T(8,128)S(1)} %add.118, f32[8,256,128]{2,1,0:T(8,128)S(1)} %convert_element_type.57, f32[8,64]{1,0:T(8,128)S(1)} %mul.144, f32[8,256]{1,0:T(8,128)S(1)} %add_rsqrt_fusion.2, f32[8,256]{1,0:T(8,128)S(1)} %get-tuple-element.24), kind=kOutput, calls=%fused_computation.19 | convolution fusion | flops 277348352 | bytes 11585536 | tf_op jit(solution)/shard_map/shqr,hrd->sqhd/dot_general | solution.py:109
  120.4 3.8 %fusion.20 = bf16[8,128,8,64]{1,3,2,0:T(8,128)(2,1)S(1)} fusion(f32[8,64,8,128]{3,1,0,2:T(8,128)S(1)} %fusion.8, f32[8,8,128,256]{3,2,1,0:T(8,128)S(1)} %bitcast.84, f32[8,8,128]{2,1,0:T(8,128)S(1)} %add.118, pred[8,256]{1,0:T(8,128)(4,1)S(1)} %fusion.45, bf16[8,128,8,128]{1,3,2,0:T(8,128)(2,1)S(1)} %copy-done.7, bf16[8,128,8,128]{1,3,2,0:T(8,128)(2,1)S(1)} %copy-done.8), kind=kOutput, calls=%fused_computation.33 | convolution fusion | flops 284164096 | bytes 15763456 | tf_op jit(solution)/shard_map/shqk,skhd->sqhd/dot_general | solution.py:106
  126.3 32.1 %all-gather.2.cloned.1.call-done = bf16[1024,1024]{0,1:T(8,128)(2,1)} async-done(((bf16[1024,512]{0,1:T(8,128)(2,1)}), bf16[1024,1024]{0,1:T(8,128)(2,1)}) %all-gather.2.cloned.1.call-update) | async-done | bytes 2097168 | tf_op jit(solution)/shard_map/all_gather | solution.py:114
  158.4 3.0 %convolution_convert_fusion = bf16[1024,512]{1,0:T(8,128)(2,1)S(1)} fusion(bf16[1024,1024]{0,1:T(8,128)(2,1)} %all-gather.2.cloned.1.call-done, bf16[1024,512]{1,0:T(8,128)(2,1)S(1)} %copy-done.16), kind=kOutput, calls=%fused_computation.44 | convolution fusion | flops 1074266112 | bytes 4194304 | tf_op jit(solution)/shard_map/dot_general | solution.py:113
  162.4 30.2 %reduce-scatter.2.cloned.1.call-done = bf16[8,512]{1,0:T(8,128)(2,1)} async-done(((bf16[64,512]{1,0:T(8,128)(2,1)}), bf16[8,512]{1,0:T(8,128)(2,1)}) %reduce-scatter.2.cloned.1.call-update) | async-done | bytes 8208 | tf_op jit(solution)/shard_map/reduce_scatter | solution.py:128
  (89 shorter events, 17.6 us)
Async XLA Ops:
  7.2 3.7 %copy-start = (bf16[1024,512]{1,0:T(8,128)(2,1)S(1)}, bf16[1024,512]{1,0:T(8,128)(2,1)}, u32[]{:S(2)}) copy-start(bf16[1024,512]{1,0:T(8,128)(2,1)} %param.13) | copy-start | bytes 3145732
  7.2 2.3 %copy-start.2 = (bf16[1024,1024]{1,0:T(8,128)(2,1)S(1)}, bf16[1024,1024]{1,0:T(8,128)(2,1)}, u32[]{:S(2)}) copy-start(bf16[1024,1024]{1,0:T(8,128)(2,1)} %param.9) | copy-start | bytes 6291460
  7.2 3.0 %copy-start.13 = (f32[1024]{0:T(1024)S(1)}, f32[1024]{0:T(1024)}, u32[]{:S(2)}) copy-start(f32[1024]{0:T(1024)} %param.10) | copy-start | bytes 12292
  7.2 100.3 %all-reduce.2.cloned.1.call-start = ((), (), s32[]{:S(2)}) async-start(), calls=%async_computation.1 | async-start | bytes 1048576 | tf_op jit(solution)/shard_map/psum | solution.py:97
  10.9 2.9 %copy-start.6 = (bf16[1024,1024]{1,0:T(8,128)(2,1)}, bf16[1024,1024]{1,0:T(8,128)(2,1)S(1)}, u32[]{:S(2)}) copy-start(bf16[1024,1024]{1,0:T(8,128)(2,1)S(1)} %fusion.6) | copy-start | bytes 6291460
  16.7 1.4 copy-start.3
  16.7 1.4 copy-start.12
  21.0 36.3 %collective-permute-start = (bf16[64,1024]{1,0:T(8,128)(2,1)S(1)}, bf16[64,1024]{1,0:T(8,128)(2,1)S(1)}, u32[]{:S(2)}, u32[]{:S(2)}) collective-permute-start(bf16[64,1024]{1,0:T(8,128)(2,1)S(1)} %copy.38), channel_id=1, source_target_pairs={{0,1},{1,4},{4,5},{5,8},{8,9},{9,12},{12,13},{2,3},{3,6},{6,7},{7,... | collective-permute-start | bytes 393224 | tf_op jit(solution)/shard_map/ppermute | solution.py:21
  24.2 33.2 %collective-permute-start.1 = (bf16[64,1024]{1,0:T(8,128)(2,1)}, bf16[64,1024]{1,0:T(8,128)(2,1)S(1)}, u32[]{:S(2)}, u32[]{:S(2)}) collective-permute-start(bf16[64,1024]{1,0:T(8,128)(2,1)} %copy.40), channel_id=1, source_target_pairs={{1,0},{4,1},{5,4},{8,5},{9,8},{12,9},{13,12},{3,2},{6,3},{7,6},{10... | collective-permute-start | bytes 393224 | tf_op jit(solution)/shard_map/ppermute | solution.py:23
  35.6 6.5 %copy-start.17 = (bf16[1024,8,64]{0,2,1:T(8,128)(2,1)S(1)}, bf16[1024,8,64]{0,2,1:T(8,128)(2,1)}, u32[]{:S(2)}) copy-start(bf16[1024,8,64]{0,2,1:T(8,128)(2,1)} %get-tuple-element.16) | copy-start | bytes 3145732
  46.6 111.8 %all-gather.2.cloned.1.call-start = ((), (), s32[]{:S(2)}) async-start(), calls=%async_computation.2 | async-start | bytes 3145728 | tf_op jit(solution)/shard_map/all_gather | solution.py:114
  54.7 2.7 %copy-start.4 = (bf16[1024,1024]{1,0:T(8,128)(2,1)S(1)}, bf16[1024,1024]{1,0:T(8,128)(2,1)}, u32[]{:S(2)}) copy-start(bf16[1024,1024]{1,0:T(8,128)(2,1)} %copy.39) | copy-start | bytes 6291460
  57.1 14.6 %copy-start.9 = (bf16[8,128,8,64]{1,3,2,0:T(8,128)(2,1)}, bf16[8,128,8,64]{1,3,2,0:T(8,128)(2,1)S(1)}, u32[]{:S(2)}) copy-start(bf16[8,128,8,64]{1,3,2,0:T(8,128)(2,1)S(1)} %copy.45) | copy-start | bytes 3145732
  61.2 4.3 %copy-start.5 = (bf16[128,8,8,128]{3,1,2,0:T(8,128)(2,1)S(1)}, bf16[128,8,8,128]{3,1,2,0:T(8,128)(2,1)}, u32[]{:S(2)}) copy-start(bf16[128,8,8,128]{3,1,2,0:T(8,128)(2,1)} %get-tuple-element.11) | copy-start | bytes 6291460
  67.5 4.3 %copy-start.7 = (bf16[8,128,8,128]{1,3,2,0:T(8,128)(2,1)S(1)}, bf16[8,128,8,128]{1,3,2,0:T(8,128)(2,1)}, u32[]{:S(2)}) copy-start(bf16[8,128,8,128]{1,3,2,0:T(8,128)(2,1)} %copy.42) | copy-start | bytes 6291460
  108.6 2.5 %copy-start.10 = (bf16[8,128,8,64]{1,3,2,0:T(8,128)(2,1)S(1)}, bf16[8,128,8,64]{1,3,2,0:T(8,128)(2,1)}, u32[]{:S(2)}) copy-start(bf16[8,128,8,64]{1,3,2,0:T(8,128)(2,1)} %copy-done.9) | copy-start | bytes 3145732
  111.2 9.2 %slice-start = ((s8[8388608]{0:T(1024)(128)(4,1)}), s8[4194304]{0:T(1024)(128)(4,1)S(1)}, s32[]{:S(2)}) async-start(s8[8388608]{0:T(1024)(128)(4,1)} %bitcast.83), calls=%async_computation.4 | async-start | bytes 8388608
  115.2 5.2 %copy-start.8 = (bf16[8,128,8,128]{1,3,2,0:T(8,128)(2,1)S(1)}, bf16[8,128,8,128]{1,3,2,0:T(8,128)(2,1)}, u32[]{:S(2)}) copy-start(bf16[8,128,8,128]{1,3,2,0:T(8,128)(2,1)} %copy.43) | copy-start | bytes 6291460
  115.2 5.2 %slice-start.1 = ((s8[8388608]{0:T(1024)(128)(4,1)}), s8[4194304]{0:T(1024)(128)(4,1)S(1)}, s32[]{:S(2)}) async-start(s8[8388608]{0:T(1024)(128)(4,1)} %bitcast.83), calls=%async_computation.5 | async-start | bytes 8388608
  124.8 1.4 copy-start.14
  124.9 33.5 %copy-start.16 = (bf16[1024,512]{1,0:T(8,128)(2,1)S(1)}, bf16[1024,512]{1,0:T(8,128)(2,1)}, u32[]{:S(2)}) copy-start(bf16[1024,512]{1,0:T(8,128)(2,1)} %param.16) | copy-start | bytes 3145732
  126.1 66.4 %reduce-scatter.2.cloned.1.call-start = ((), (), s32[]{:S(2)}) async-start(), calls=%async_computation.3 | async-start | bytes 73728 | tf_op jit(solution)/shard_map/reduce_scatter | solution.py:128
  158.4 35.6 %copy-start.1 = (bf16[1024,512]{1,0:T(8,128)(2,1)S(1)}, bf16[1024,512]{1,0:T(8,128)(2,1)}, u32[]{:S(2)}) copy-start(bf16[1024,512]{1,0:T(8,128)(2,1)} %param.13) | copy-start | bytes 3145732
  161.4 32.6 %copy-start.11 = (bf16[1024,512]{1,0:T(8,128)(2,1)}, bf16[1024,512]{1,0:T(8,128)(2,1)S(1)}, u32[]{:S(2)}) copy-start(bf16[1024,512]{1,0:T(8,128)(2,1)S(1)} %convolution_convert_fusion) | copy-start | bytes 3145732
  (1 other events, 1.2 us)
Sparse Core Ops, SparseCore 0:
  46.8 60.7 all-reduce.1
  126.3 32.0 all-gather.1
  162.5 30.0 reduce-scatter.1
where the time goes:
time: 201 us; the launch traced here: 200 us
  waiting for transfers between devices  90.6 us (45%)
  matrix products  46.4 us (23%)
  local copies, waits for them, and re-layouts  31.1 us (15%)
  between operations  14.2 us (7%)
  other arithmetic  14 us (7%)
  starting transfers between devices  4.17 us (2%)
    all_gather x1, waiting for transfers between devices, per_device(): lax.all_gather(heads_out, 'head', axis=1, tiled=True)  32.1 us
    reduce_scatter x1, waiting for transfers between devices, per_device(): lax.psum_scatter(partial_sums.astype(jnp.bfloat16), ('seq', 'rep'), scatt...  30.2 us
    psum x1, waiting for transfers between devices, per_device(): lax.psum(numerator.astype(jnp.bfloat16), ('seq', 'rep')).astype(jnp.float32)  28.3 us
    dot_general x1, matrix products, per_device(): logits = jnp.dot(normed, proj_weight, preferred_element_type=jnp.float32)  9.95 us
    slice x2, local copies, waits for them, and re-layouts, per_device(): window = jnp.concatenate([blocks[:-1], blocks[1:]], axis=1)  8.56 us
    dot_general x1, matrix products, per_device(): jnp.einsum('sqhd,skhd->shqk', query_blocks, window[..., :DH], preferred_e...  7.46 us
    unnamed x43, local copies, waits for them, and re-layouts  6.76 us
    reshape x1, local copies, waits for them, and re-layouts, per_device(): jnp.exp(capped(logits)).astype(jnp.bfloat16)  6.49 us
  transfers between devices with their start and end apart: 5, of which 3 were waited for; matrix products, arithmetic and copies ran while one was open for 27% of the time, Pallas kernels for 0%

commit v1 on v0

--- a/solution.py
+++ b/solution.py
@@ -2,12 +2,17 @@
 import jax.numpy as jnp
 from jax import lax
 from jax.sharding import PartitionSpec as P
+from jax.lax import all_gather
 
 DH = 64
 R = 256
 SEG = 128
 softcap = 5.0
 epsilon = 1e-05
+
+
+def run_store(inp, mesh_dim):
+    return all_gather(inp, mesh_dim).sum(axis=0)
 
 
 def with_halo(cells, sides, width):
@@ -94,7 +99,9 @@
         "sqhd,skhd->shqk", query_blocks, window[..., :DH], preferred_element_type=jnp.float32
     )
     near_exp = jnp.where(inside[:, None, None, :], jnp.exp(capped(near_scores * DH ** (-0.5))), 0.0)
-    total_numer = lax.psum(numerator.astype(jnp.bfloat16), ("seq", "rep")).astype(jnp.float32)
+    total_numer = run_store(numerator.astype(jnp.bfloat16), mesh_dim=("seq", "rep")).astype(
+        jnp.float32
+    )
     land_pairs = finish(total_numer, gain_rows)
     far_scores = jnp.einsum(
         "sqhd,hrd->shqr", query_blocks, land_pairs[..., :DH], preferred_element_type=jnp.float32

time: 201 us -> 181 us (0.900)
  waiting for transfers between devices: 90.6 us -> 72.4 us
    psum x1 -> x0, waiting for transfers between devices: 28.3 us -> none  [per_device(): lax.psum(numerator.astype(jnp.bfloat16), ('seq', 'rep')).astype(jnp.float32)]
    all_gather x0 -> x1, waiting for transfers between devices: none -> 10.3 us  [run_store(): return all_gather(inp, mesh_dim).sum(axis=0)]
    dot_general x1, matrix products: 9.95 us -> 6.89 us  [per_device(): logits = jnp.dot(normed, proj_weight, preferred_element_type=jnp.float32)]
    reduce_sum x0 -> x1, other arithmetic: none -> 2.94 us  [run_store(): return all_gather(inp, mesh_dim).sum(axis=0)]
    unnamed x43 -> x45, local copies, waits for them, and re-layouts: 6.76 us -> 6.75 us
  transfers between devices with their start and end apart: 5 -> 5, of which waited for: 3 -> 3; matrix products, arithmetic and copies ran while one was open for 27% -> 20% of each run, Pallas kernels for 0% -> 0%
where the time goes in v1:
time: 181 us
  waiting for transfers between devices  72.4 us (40%)
  matrix products  44.9 us (25%)
  local copies, waits for them, and re-layouts  31 us (17%)
  other arithmetic  14.4 us (8%)
  between operations  14.2 us (8%)
  starting transfers between devices  3.94 us (2%)
    all_gather x1, waiting for transfers between devices, per_device(): lax.all_gather(heads_out, 'head', axis=1, tiled=True)  31.8 us
    reduce_scatter x1, waiting for transfers between devices, per_device(): lax.psum_scatter(partial_sums.astype(jnp.bfloat16), ('seq', 'rep'), scatt...  30.2 us
    all_gather x1, waiting for transfers between devices, run_store(): return all_gather(inp, mesh_dim).sum(axis=0)  10.3 us
    slice x2, local copies, waits for them, and re-layouts, per_device(): window = jnp.concatenate([blocks[:-1], blocks[1:]], axis=1)  8.61 us
    dot_general x1, matrix products, per_device(): jnp.einsum('sqhd,skhd->shqk', query_blocks, window[..., :DH], preferred_e...  7.47 us
    dot_general x1, matrix products, per_device(): logits = jnp.dot(normed, proj_weight, preferred_element_type=jnp.float32)  6.89 us
    unnamed x45, local copies, waits for them, and re-layouts  6.75 us
    reshape x1, local copies, waits for them, and re-layouts, per_device(): jnp.exp(capped(logits)).astype(jnp.bfloat16)  6.4 us
  transfers between devices with their start and end apart: 5, of which 3 were waited for; matrix products, arithmetic and copies ran while one was open for 20% of the time, Pallas kernels for 0%

profile of v1, /device:TPU:0, one launch (start us, length us, event | category | flops | bytes accessed | tf_op | source)
XLA Modules:
  0.0 180.8 jit_solution(7487133293092711144)
XLA Ops:
  7.2 2.1 %convert_reduce_fusion = f32[1024]{0:T(1024)S(1)} fusion(bf16[1024,1024]{1,0:T(8,128)(2,1)} %param.9), kind=kLoop, calls=%fused_computation.9 | loop fusion | flops 2096128 | bytes 2101248 | tf_op jit(solution)/shard_map/reduce_sum | solution.py:36
  10.9 2.3 %bitcast_convert_fusion = (bf16[1024,8,64]{0,2,1:T(8,128)(2,1)}, f32[1024,512]{0,1:T(8,128)S(1)}) fusion(bf16[1024,1024]{1,0:T(8,128)(2,1)S(1)} %fusion.6, bf16[1024,512]{1,0:T(8,128)(2,1)S(1)} %copy-done), kind=kOutput, calls=%fused_computation.34 | convolution fusion | flops 1074266112 | bytes 6291456 | tf_op jit(solution)/shard_map/dot_general | solution.py:74
  13.2 3.2 %bitcast_convert_fusion.1 = (bf16[1024,8,64]{0,2,1:T(8,128)(2,1)}, f32[1024,512]{0,1:T(8,128)}) fusion(bf16[1024,1024]{1,0:T(8,128)(2,1)S(1)} %fusion.6, bf16[1024,512]{1,0:T(8,128)(2,1)S(1)} %copy-done.17), kind=kOutput, calls=%fused_computation.37 | convolution fusion | flops 1074266112 | bytes 6291456 | tf_op jit(solution)/shard_map/dot_general | solution.py:71
  16.4 6.9 %exponential_convert_fusion = bf16[1024,2048]{1,0:T(8,128)(2,1)} fusion(bf16[1024,1024]{1,0:T(8,128)(2,1)S(1)} %fusion.6, bf16[1024,2048]{1,0:T(8,128)(2,1)S(1)} %copy-done.16), kind=kOutput, calls=%fused_computation.5 | convolution fusion | flops 4301258752 | bytes 10485760 | tf_op jit(solution)/shard_map/dot_general | solution.py:83
  23.3 6.4 %copy.69 = bf16[1024,2048]{0,1:T(8,128)(2,1)} copy(bf16[1024,2048]{1,0:T(8,128)(2,1)} %exponential_convert_fusion) | data formatting | bytes 8388608 | tf_op jit(solution)/shard_map/reshape | solution.py:84
  29.7 4.8 %fusion.23 = bf16[8,256,128]{2,1,0:T(8,128)(2,1)} fusion(bf16[1024,8,256]{0,2,1:T(8,128)(2,1)} %bitcast.80, bf16[1024,8,64]{0,2,1:T(8,128)(2,1)} %get-tuple-element.16, bf16[1024,8,64]{0,2,1:T(8,128)(2,1)} %get-tuple-element.18), kind=kOutput, calls=%fused_computation.46 | convolution fusion | flops 541327360 | bytes 6815744 | tf_op jit(solution)/shard_map/nhr,nhe->hre/dot_general | solution.py:85
  38.5 2.4 %collective-permute-start = (bf16[64,1024]{1,0:T(8,128)(2,1)S(1)}, bf16[64,1024]{1,0:T(8,128)(2,1)S(1)}, u32[]{:S(2)}, u32[]{:S(2)}) collective-permute-start(bf16[64,1024]{1,0:T(8,128)(2,1)S(1)} %copy.49), channel_id=1, source_target_pairs={{0,1},{1,4},{4,5},{5,8},{8,9},{9,12},{12,13},{2,3},{3,6},{6,7},{7,... | collective-permute-start | bytes 393224 | tf_op jit(solution)/shard_map/ppermute | solution.py:26
  43.1 2.6 %copy.50 = bf16[1024,1024]{1,0:T(8,128)(2,1)} copy(bf16[1024,1024]{0,1:T(8,128)(2,1)S(1)} %bitcast.76) | data formatting | bytes 4194304 | tf_op jit(solution)/shard_map/convert_element_type | solution.py:81
  45.7 3.2 %convolution_convert_fusion.1 = bf16[1024,512]{1,0:T(8,128)(2,1)S(1)} fusion(bf16[1024,1024]{1,0:T(8,128)(2,1)} %copy-done.6, bf16[1024,512]{1,0:T(8,128)(2,1)} %param.11), kind=kOutput, calls=%fused_computation.45 | convolution fusion | flops 1074266112 | bytes 4194304 | tf_op jit(solution)/shard_map/dot_general | solution.py:69
  48.9 2.1 %reshape.141 = bf16[8,128,8,64]{3,2,1,0:T(8,128)(2,1)} reshape(bf16[1024,512]{1,0:T(8,128)(2,1)S(1)} %convolution_convert_fusion.1) | data formatting | bytes 2097152 | tf_op jit(solution)/shard_map/reshape;reshape | solution.py:97
  51.0 2.4 %copy.56 = bf16[8,128,8,64]{1,3,2,0:T(8,128)(2,1)S(1)} copy(bf16[8,128,8,64]{3,2,1,0:T(8,128)(2,1)} %reshape.141) | data formatting | bytes 2097152 | tf_op jit(solution)/shard_map/reshape;reshape | solution.py:97
  53.7 2.0 %fusion.15 = (bf16[128,8,8,128]{3,1,2,0:T(8,128)(2,1)S(1)}, bf16[128,8,8,128]{3,1,2,0:T(8,128)(2,1)}) fusion(bf16[1024,1024]{1,0:T(8,128)(2,1)S(1)} %copy-done.4, bf16[64,1024]{1,0:T(8,128)(2,1)S(1)} %collective-permute-done, bf16[64,1024]{1,0:T(8,128)(2,1)S(1)} %collective-permute-done.1), kind=kLoop, calls=%fused_computation.27 | loop fusion | flops 8388608 | bytes 6553600
  57.6 4.3 %copy.53 = bf16[8,128,8,128]{1,3,2,0:T(8,128)(2,1)} copy(bf16[8,128,8,128]{3,2,1,0:T(8,128)(2,1)} %bitcast.77) | data formatting | bytes 4194304 | tf_op jit(solution)/shard_map/slice | solution.py:92
  61.9 2.0 %copy.76 = bf16[128,8,8,128]{3,2,1,0:T(8,128)(2,1)} copy(bf16[128,8,8,128]{3,1,2,0:T(8,128)(2,1)S(1)} %copy-done.5) | data formatting | bytes 4194304
  63.8 4.3 %copy.54 = bf16[8,128,8,128]{1,3,2,0:T(8,128)(2,1)} copy(bf16[8,128,8,128]{3,2,1,0:T(8,128)(2,1)} %bitcast.78) | data formatting | bytes 4194304 | tf_op jit(solution)/shard_map/slice | solution.py:92
  68.2 7.5 %fusion.1 = (f32[8,8,128]{2,1,0:T(8,128)S(1)}, f32[8,8,128,256]{3,2,1,0:T(8,128)}) fusion(pred[8,256]{1,0:T(8,128)(4,1)S(1)} %fusion.45, bf16[8,128,8,64]{1,3,2,0:T(8,128)(2,1)S(1)} %copy.56, bf16[8,128,8,128]{1,3,2,0:T(8,128)(2,1)} %copy.54, bf16[8,128,8,128]{1,3,2,0:T(8,128)(2,1)S(1)} %copy-done.7), kind=kOutput, calls=%fused_computation.7 | convolution fusion | flops 281010176 | bytes 13666304 | tf_op jit(solution)/shard_map/sqhd,skhd->shqk/dot_general | solution.py:98
  75.6 10.3 %all-gather.6.cloned.1.call-done = bf16[64,256,128]{2,1,0:T(8,128)(2,1)} async-done(((bf16[8,256,128]{2,1,0:T(8,128)(2,1)}), bf16[64,256,128]{2,1,0:T(8,128)(2,1)}) %all-gather.6.cloned.1.call-update) | async-done | bytes 4194320 | tf_op jit(solution)/shard_map/all_gather | solution.py:15
  85.9 2.9 %reduce_sum.127 = bf16[8,256,128]{2,1,0:T(8,128)(2,1)S(1)} reduce(bf16[8,8,256,128]{3,2,1,0:T(8,128)(2,1)} %bitcast.79, bf16[]{:T(256)} %constant.58.clone.1), dimensions={0}, to_apply=%region_7.8 | reduce | flops 1835008 | bytes 4718594 | tf_op jit(solution)/shard_map/reduce_sum | solution.py:15
  91.5 3.9 %bitcast_reduce_fusion = (f32[8,8,128]{2,1,0:T(8,128)S(1)}, f32[8,256,8,128]{1,3,0,2:T(8,128)S(1)}) fusion(bf16[8,128,8,64]{1,3,2,0:T(8,128)(2,1)S(1)} %copy-done.11, f32[8,256,128]{2,1,0:T(8,128)S(1)} %convert_element_type.59, f32[8,64]{1,0:T(8,128)S(1)} %mul.138, f32[8,256]{1,0:T(8,128)S(1)} %add_rsqrt_fusion.3, f32[8,256]{1,0:T(8,128)S(1)} %get-tuple-element.25), kind=kOutput, calls=%fused_computation.1 | convolution fusion | flops 275243008 | bytes 10536960 | tf_op jit(solution)/shard_map/sqhd,hrd->shqr/dot_general | solution.py:106
  95.5 5.2 %fusion.8 = f32[8,64,8,128]{3,1,0,2:T(8,128)S(1)} fusion(f32[8,256,8,128]{1,3,0,2:T(8,128)S(1)} %get-tuple-element.23, f32[8,8,128]{2,1,0:T(8,128)S(1)} %add.116, f32[8,256,128]{2,1,0:T(8,128)S(1)} %convert_element_type.59, f32[8,64]{1,0:T(8,128)S(1)} %mul.144, f32[8,256]{1,0:T(8,128)S(1)} %add_rsqrt_fusion.2, f32[8,256]{1,0:T(8,128)S(1)} %get-tuple-element.24), kind=kOutput, calls=%fused_computation.19 | convolution fusion | flops 277348352 | bytes 11585536 | tf_op jit(solution)/shard_map/shqr,hrd->sqhd/dot_general | solution.py:116
  100.7 4.0 %fusion.20 = bf16[8,128,8,64]{1,3,2,0:T(8,128)(2,1)S(1)} fusion(f32[8,64,8,128]{3,1,0,2:T(8,128)S(1)} %fusion.8, f32[8,8,128,256]{3,2,1,0:T(8,128)S(1)} %bitcast.86, f32[8,8,128]{2,1,0:T(8,128)S(1)} %add.116, pred[8,256]{1,0:T(8,128)(4,1)S(1)} %fusion.45, bf16[8,128,8,128]{1,3,2,0:T(8,128)(2,1)S(1)} %copy-done.8, bf16[8,128,8,128]{1,3,2,0:T(8,128)(2,1)S(1)} %copy-done.9), kind=kOutput, calls=%fused_computation.33 | convolution fusion | flops 284164096 | bytes 15763456 | tf_op jit(solution)/shard_map/shqk,skhd->sqhd/dot_general | solution.py:113
  106.8 31.8 %all-gather.4.cloned.1.call-done = bf16[1024,1024]{0,1:T(8,128)(2,1)} async-done(((bf16[1024,512]{0,1:T(8,128)(2,1)}), bf16[1024,1024]{0,1:T(8,128)(2,1)}) %all-gather.4.cloned.1.call-update) | async-done | bytes 2097168 | tf_op jit(solution)/shard_map/all_gather | solution.py:121
  138.7 3.0 %convolution_convert_fusion = bf16[1024,512]{1,0:T(8,128)(2,1)S(1)} fusion(bf16[1024,1024]{0,1:T(8,128)(2,1)} %all-gather.4.cloned.1.call-done, bf16[1024,512]{1,0:T(8,128)(2,1)S(1)} %copy-done.18), kind=kOutput, calls=%fused_computation.44 | convolution fusion | flops 1074266112 | bytes 4194304 | tf_op jit(solution)/shard_map/dot_general | solution.py:120
  142.7 30.2 %reduce-scatter.2.cloned.1.call-done = bf16[8,512]{1,0:T(8,128)(2,1)} async-done(((bf16[64,512]{1,0:T(8,128)(2,1)}), bf16[8,512]{1,0:T(8,128)(2,1)}) %reduce-scatter.2.cloned.1.call-update) | async-done | bytes 8208 | tf_op jit(solution)/shard_map/reduce_scatter | solution.py:135
  (92 shorter events, 17.0 us)
Async XLA Ops:
  7.2 3.7 %copy-start = (bf16[1024,512]{1,0:T(8,128)(2,1)S(1)}, bf16[1024,512]{1,0:T(8,128)(2,1)}, u32[]{:S(2)}) copy-start(bf16[1024,512]{1,0:T(8,128)(2,1)} %param.13) | copy-start | bytes 3145732
  7.2 2.3 %copy-start.2 = (bf16[1024,1024]{1,0:T(8,128)(2,1)S(1)}, bf16[1024,1024]{1,0:T(8,128)(2,1)}, u32[]{:S(2)}) copy-start(bf16[1024,1024]{1,0:T(8,128)(2,1)} %param.9) | copy-start | bytes 6291460
  7.2 3.0 %copy-start.14 = (f32[1024]{0:T(1024)S(1)}, f32[1024]{0:T(1024)}, u32[]{:S(2)}) copy-start(f32[1024]{0:T(1024)} %param.10) | copy-start | bytes 12292
  7.2 78.7 %all-gather.6.cloned.1.call-start = ((), (), s32[]{:S(2)}) async-start(), calls=%async_computation.3 | async-start | bytes 4718592 | tf_op jit(solution)/shard_map/all_gather | solution.py:15
  10.9 5.5 %copy-start.6 = (bf16[1024,1024]{1,0:T(8,128)(2,1)}, bf16[1024,1024]{1,0:T(8,128)(2,1)S(1)}, u32[]{:S(2)}) copy-start(bf16[1024,1024]{1,0:T(8,128)(2,1)S(1)} %fusion.6) | copy-start | bytes 6291460
  10.9 2.3 %copy-start.17 = (bf16[1024,512]{1,0:T(8,128)(2,1)S(1)}, bf16[1024,512]{1,0:T(8,128)(2,1)}, u32[]{:S(2)}) copy-start(bf16[1024,512]{1,0:T(8,128)(2,1)} %param.12) | copy-start | bytes 3145732
  13.2 3.2 %copy-start.16 = (bf16[1024,2048]{1,0:T(8,128)(2,1)S(1)}, bf16[1024,2048]{1,0:T(8,128)(2,1)}, u32[]{:S(2)}) copy-start(bf16[1024,2048]{1,0:T(8,128)(2,1)} %param.14) | copy-start | bytes 12582916
  29.7 4.9 %copy-start.13 = (f32[4,512]{1,0:T(4,128)S(1)}, f32[4,512]{1,0:T(4,128)}, u32[]{:S(2)}) copy-start(f32[4,512]{1,0:T(4,128)} %param.15) | copy-start | bytes 24580
  34.6 104.1 %all-gather.4.cloned.1.call-start = ((), (), s32[]{:S(2)}) async-start(), calls=%async_computation.1 | async-start | bytes 3145728 | tf_op jit(solution)/shard_map/all_gather | solution.py:121
  38.5 15.1 %collective-permute-start = (bf16[64,1024]{1,0:T(8,128)(2,1)S(1)}, bf16[64,1024]{1,0:T(8,128)(2,1)S(1)}, u32[]{:S(2)}, u32[]{:S(2)}) collective-permute-start(bf16[64,1024]{1,0:T(8,128)(2,1)S(1)} %copy.49), channel_id=1, source_target_pairs={{0,1},{1,4},{4,5},{5,8},{8,9},{9,12},{12,13},{2,3},{3,6},{6,7},{7,... | collective-permute-start | bytes 393224 | tf_op jit(solution)/shard_map/ppermute | solution.py:26
  41.7 12.0 %collective-permute-start.1 = (bf16[64,1024]{1,0:T(8,128)(2,1)}, bf16[64,1024]{1,0:T(8,128)(2,1)S(1)}, u32[]{:S(2)}, u32[]{:S(2)}) collective-permute-start(bf16[64,1024]{1,0:T(8,128)(2,1)} %copy.51), channel_id=1, source_target_pairs={{1,0},{4,1},{5,4},{8,5},{9,8},{12,9},{13,12},{3,2},{6,3},{7,6},{10... | collective-permute-start | bytes 393224 | tf_op jit(solution)/shard_map/ppermute | solution.py:28
  51.0 2.7 %copy-start.4 = (bf16[1024,1024]{1,0:T(8,128)(2,1)S(1)}, bf16[1024,1024]{1,0:T(8,128)(2,1)}, u32[]{:S(2)}) copy-start(bf16[1024,1024]{1,0:T(8,128)(2,1)} %copy.50) | copy-start | bytes 6291460
  53.4 14.7 %copy-start.10 = (bf16[8,128,8,64]{1,3,2,0:T(8,128)(2,1)}, bf16[8,128,8,64]{1,3,2,0:T(8,128)(2,1)S(1)}, u32[]{:S(2)}) copy-start(bf16[8,128,8,64]{1,3,2,0:T(8,128)(2,1)S(1)} %copy.56) | copy-start | bytes 3145732
  57.6 4.3 %copy-start.5 = (bf16[128,8,8,128]{3,1,2,0:T(8,128)(2,1)S(1)}, bf16[128,8,8,128]{3,1,2,0:T(8,128)(2,1)}, u32[]{:S(2)}) copy-start(bf16[128,8,8,128]{3,1,2,0:T(8,128)(2,1)} %get-tuple-element.11) | copy-start | bytes 6291460
  63.8 4.3 %copy-start.7 = (bf16[8,128,8,128]{1,3,2,0:T(8,128)(2,1)S(1)}, bf16[8,128,8,128]{1,3,2,0:T(8,128)(2,1)}, u32[]{:S(2)}) copy-start(bf16[8,128,8,128]{1,3,2,0:T(8,128)(2,1)} %copy.53) | copy-start | bytes 6291460
  89.0 2.5 %copy-start.11 = (bf16[8,128,8,64]{1,3,2,0:T(8,128)(2,1)S(1)}, bf16[8,128,8,64]{1,3,2,0:T(8,128)(2,1)}, u32[]{:S(2)}) copy-start(bf16[8,128,8,64]{1,3,2,0:T(8,128)(2,1)} %copy-done.10) | copy-start | bytes 3145732
  91.5 9.2 %slice-start = ((s8[8388608]{0:T(1024)(128)(4,1)}), s8[4194304]{0:T(1024)(128)(4,1)S(1)}, s32[]{:S(2)}) async-start(s8[8388608]{0:T(1024)(128)(4,1)} %bitcast.85), calls=%async_computation.4 | async-start | bytes 8388608
  95.5 5.2 %copy-start.8 = (bf16[8,128,8,128]{1,3,2,0:T(8,128)(2,1)S(1)}, bf16[8,128,8,128]{1,3,2,0:T(8,128)(2,1)}, u32[]{:S(2)}) copy-start(bf16[8,128,8,128]{1,3,2,0:T(8,128)(2,1)} %copy.53) | copy-start | bytes 6291460
  95.5 5.2 %copy-start.9 = (bf16[8,128,8,128]{1,3,2,0:T(8,128)(2,1)S(1)}, bf16[8,128,8,128]{1,3,2,0:T(8,128)(2,1)}, u32[]{:S(2)}) copy-start(bf16[8,128,8,128]{1,3,2,0:T(8,128)(2,1)} %copy.54) | copy-start | bytes 6291460
  95.5 5.2 %slice-start.1 = ((s8[8388608]{0:T(1024)(128)(4,1)}), s8[4194304]{0:T(1024)(128)(4,1)S(1)}, s32[]{:S(2)}) async-start(s8[8388608]{0:T(1024)(128)(4,1)} %bitcast.85), calls=%async_computation.5 | async-start | bytes 8388608
  105.4 33.3 %copy-start.18 = (bf16[1024,512]{1,0:T(8,128)(2,1)S(1)}, bf16[1024,512]{1,0:T(8,128)(2,1)}, u32[]{:S(2)}) copy-start(bf16[1024,512]{1,0:T(8,128)(2,1)} %param.16) | copy-start | bytes 3145732
  106.7 66.2 %reduce-scatter.2.cloned.1.call-start = ((), (), s32[]{:S(2)}) async-start(), calls=%async_computation.2 | async-start | bytes 73728 | tf_op jit(solution)/shard_map/reduce_scatter | solution.py:135
  138.7 35.6 %copy-start.1 = (bf16[1024,512]{1,0:T(8,128)(2,1)S(1)}, bf16[1024,512]{1,0:T(8,128)(2,1)}, u32[]{:S(2)}) copy-start(bf16[1024,512]{1,0:T(8,128)(2,1)} %param.13) | copy-start | bytes 3145732
  141.6 32.6 %copy-start.12 = (bf16[1024,512]{1,0:T(8,128)(2,1)}, bf16[1024,512]{1,0:T(8,128)(2,1)S(1)}, u32[]{:S(2)}) copy-start(bf16[1024,512]{1,0:T(8,128)(2,1)S(1)} %convolution_convert_fusion) | copy-start | bytes 3145732
  (2 other events, 2.9 us)
Sparse Core Ops, SparseCore 0:
  34.7 51.1 all-gather.5
  106.8 31.8 all-gather.3
  142.8 30.0 reduce-scatter.1
